TPU v7x, 128 devices: a whole 4x4x4 slice. The times are simulated.
128 devices in a mesh: row: 16 (over y, x), col: 8 (over z, core).
Axes of the slice: x: 4, y: 4, z: 4, core: 2. Of those that a mesh axis runs over, the one named last changes fastest.
Arguments:
- front_first: float32 [16, 4, 128, 8, 8, 128], P('row', None, None, 'col'), as said below
- front_second: float32 [16, 4, 128, 8, 8, 128], P('row', None, None, 'col'), as said below
- front_third: float32 [16, 4, 128, 8, 8, 128], P('row', None, None, 'col'), as said below
- map_second: int32 [60], replicated, may hold values from 0 to 63, as said below
- map_third: int32 [60], replicated, may hold values from 0 to 63, as said below
Outputs:
- lower_first: float32 [16, 4, 128, 512], P('row')
- lower_second: float32 [16, 4, 128, 512], P('row')
- lower_third: float32 [16, 4, 128, 512], P('row')
- schur_third: float32 [16, 4, 128, 8, 8, 128], P('row', None, None, 'col')
Inputs may be any that keep to these rules, and one draw needn't show every extreme that they name: `map_second`: strictly increasing; the first entry is 0 and the last is 63. `map_third`: strictly increasing; the first entry is 0 and the last is 63. `front_first`: symmetric positive definite. `front_second`: symmetric positive definite. `front_third`: symmetric positive definite.
All inputs are finite; a program needn't handle non-finite values.
Results may differ from a plain program's by a relative error of at most 0.00012.
Values sent between devices are 32-bit elements; how exact they have to be, the bound alone decides.
No kernel may reach another device: no remote copies, remote signals or barrier semaphores. Data moves between devices by JAX's collectives and lax.ppermute only.
A program may use at most 128 MiB of HBM per device.

v0:
```python
import jax
import jax.numpy as jnp
from jax import lax
from jax.sharding import PartitionSpec as P

TILE = 128
PANEL = 512
PIVOTS = 512


def shifted(value, axis, steps):
    count = lax.axis_size(axis)
    pairs = [(source, (source + steps) % count) for source in range(count)]
    return lax.ppermute(value, axis, pairs)


def spread(block, axis, source):
    block = jnp.where(lax.axis_index(axis) == source, block, jnp.zeros_like(block))
    return lax.psum(block, axis)


def shift_rows(block_data, amount):
    return shifted(block_data, "row", amount)


def shift_cols(block_data, amount):
    return shifted(block_data, "col", amount)


def relocate(block_data, block_map, axis_dim, count, index, shifter):
    pivot_blocks = PIVOTS // TILE
    local_tiles = block_data.shape[axis_dim]
    child_start = jnp.arange(block_map.shape[0], dtype=jnp.int32) + pivot_blocks
    displacement = child_start - block_map
    local_pos = jnp.arange(local_tiles, dtype=jnp.int32) * count + index
    for bit_index in reversed(range(pivot_blocks.bit_length())):
        stride = 1 << bit_index
        high_part = displacement >> bit_index + 1 << bit_index + 1
        where_now = child_start - high_part
        moving_now = displacement >> bit_index & 1 == 1
        moving = jnp.any((where_now[None, :] == local_pos[:, None]) & moving_now[None, :], axis=1)
        if axis_dim == 0:
            tile_mask = moving[:, None, None, None]
        else:
            tile_mask = moving[None, None, :, None]
        sending = jnp.where(tile_mask, block_data, 0.0)
        staying = jnp.where(tile_mask, 0.0, block_data)
        full_turns = stride // count
        remainder = stride % count
        arrived = shifter(sending, count - remainder)
        roll_amount = full_turns + (index + remainder >= count).astype(jnp.int32)
        arrived = jnp.roll(arrived, -roll_amount, axis=axis_dim)
        block_data = staying + arrived
    return block_data


def per_device(front_first, front_second, front_third, map_second, map_third):
    row_count = lax.axis_size("row")
    col_count = lax.axis_size("col")
    row_index = lax.axis_index("row")
    col_index = lax.axis_index("col")
    tiles_row = front_first.shape[1]
    tile_size = front_first.shape[2]
    tiles_col = front_first.shape[4]
    panel_tiles = PANEL // tile_size
    row_logical = (
        (jnp.arange(tiles_row, dtype=jnp.int32) * row_count + row_index)[:, None] * tile_size
        + jnp.arange(tile_size, dtype=jnp.int32)[None, :]
    ).reshape(-1)
    col_logical = (
        (jnp.arange(tiles_col, dtype=jnp.int32) * col_count + col_index)[:, None] * tile_size
        + jnp.arange(tile_size, dtype=jnp.int32)[None, :]
    ).reshape(-1)

    def local_form(front):
        return front.reshape(tiles_row, tile_size, tiles_col, tile_size)

    def factor_local(matrix):
        first_tile = 0 // tile_size
        pieces = []
        for member in range(panel_tiles):
            global_col = first_tile + member
            pieces.append(
                spread(matrix[:, :, global_col // col_count, :], "col", global_col % col_count)
            )
        panel_cols = jnp.stack(pieces, axis=2).reshape(tiles_row * tile_size, PANEL)
        panel_tiled = panel_cols.reshape(tiles_row, tile_size, PANEL)
        diagonal_parts = []
        for member in range(panel_tiles):
            global_row = first_tile + member
            diagonal_parts.append(
                spread(panel_tiled[global_row // row_count], "row", global_row % row_count)
            )
        diagonal = jnp.concatenate(diagonal_parts, axis=0)
        factor_block = jnp.linalg.cholesky(diagonal)
        inverse = lax.linalg.triangular_solve(
            factor_block, jnp.eye(PANEL, dtype=jnp.float32), left_side=True, lower=True
        )
        lower_panel = jnp.dot(
            panel_cols,
            inverse.T,
            precision=lax.Precision.HIGHEST,
            preferred_element_type=jnp.float32,
        )
        lower_panel = jnp.where((row_logical >= 0)[:, None], lower_panel, 0.0)
        received = []
        for member in range(row_count // col_count):
            got = spread(lower_panel, "row", member * col_count + col_index)
            received.append(got.reshape(tiles_row, tile_size, PANEL))
        column_side = jnp.stack(received, axis=1).reshape(tiles_col * tile_size, PANEL)
        update = jnp.dot(
            lower_panel,
            column_side.T,
            precision=lax.Precision.HIGHEST,
            preferred_element_type=jnp.float32,
        )
        matrix = matrix - update.reshape(tiles_row, tile_size, tiles_col, tile_size)
        row_keep = (row_logical >= PIVOTS).reshape(tiles_row, tile_size)
        col_keep = (col_logical >= PIVOTS).reshape(tiles_col, tile_size)
        schur = jnp.where(row_keep[:, :, None, None] & col_keep[None, None, :, :], matrix, 0.0)
        return (lower_panel, schur)

    def extend_local(parent, schur, block_map):
        moved = relocate(schur, block_map, 0, row_count, row_index, shift_rows)
        moved = relocate(moved, block_map, 2, col_count, col_index, shift_cols)
        return parent + moved

    lower_first, schur_first = factor_local(local_form(front_first))
    lower_second, schur_second = factor_local(
        extend_local(local_form(front_second), schur_first, map_second)
    )
    lower_third, schur_third = factor_local(
        extend_local(local_form(front_third), schur_second, map_third)
    )
    out_shape = (1, tiles_row, tile_size, PIVOTS)
    return (
        lower_first.reshape(out_shape),
        lower_second.reshape(out_shape),
        lower_third.reshape(out_shape),
        schur_third.reshape(1, tiles_row, tile_size, 1, tiles_col, tile_size),
    )


def solution(mesh):
    return jax.shard_map(
        per_device,
        mesh=mesh,
        in_specs=(
            P("row", None, None, "col", None, None),
            P("row", None, None, "col", None, None),
            P("row", None, None, "col", None, None),
            P(),
            P(),
        ),
        out_specs=(
            P("row", None, None, None),
            P("row", None, None, None),
            P("row", None, None, None),
            P("row", None, None, "col", None, None),
        ),
        check_vma=False,
    )
```

profile of v0, /device:TPU:0, one launch (start us, length us, event | category | flops | bytes accessed | tf_op | source)
XLA Modules:
  0.0 1831.1 jit_solution(12885181710065170013)
XLA Ops:
  10.3 66.3 %all-reduce.36.cloned.1.call-done = (f32[4,128,1,128]{3,1,2,0:T(8,128)}, f32[4,128,1,128]{3,1,2,0:T(8,128)}, f32[4,128,1,128]{3,1,2,0:T(8,128)}, f32[4,128,1,128]{3,1,2,0:T(8,128)}) async-done(((f32[4,128,1,128]{3,1,2,0:T(8,128)}, f32[4,128,1,128]{3,1,2,0:T(8,128)}, f32[4,128,1,128]{3,1,2,0:T(8,128)}, f32[4,128,1,128]{3,1,2,0:T(8,128)}), (f32[4,128,1,128]{3,1,2,0:T(8,128)}, f32[4,128,1,128]{3,1,2,0:T(8,128)}, ...) | async-done | bytes 1048592 | tf_op jit(solution)/shard_map/psum | solution.py:19
  85.9 84.5 %all-reduce.30.cloned.1.call-done = (f32[128,512]{0,1:T(8,128)}, f32[128,512]{0,1:T(8,128)}, f32[128,512]{0,1:T(8,128)}, f32[128,512]{0,1:T(8,128)}) async-done(((f32[128,512]{0,1:T(8,128)}, f32[128,512]{0,1:T(8,128)}, f32[128,512]{0,1:T(8,128)}, f32[128,512]{0,1:T(8,128)}), (f32[128,512]{0,1:T(8,128)}, f32[128,512]{0,1:T(8,128)}, f32[128,512]{0,1:T(8,128)}, ...) | async-done | bytes 1048592 | tf_op jit(solution)/shard_map/psum | solution.py:19
  175.9 11.7 cholesky.374
  246.4 11.9 cholesky.431
  271.2 39.3 %custom-call.34 = f32[4,128,128]{1,2,0:T(8,128)S(1)} custom-call(f32[4,128,128]{2,1,0:T(8,128)S(1)} %get-tuple-element.28), custom_call_target="InvertDiagBlocksLowerTriangular" | custom-call | tf_op jit(solution)/shard_map/triangular_solve/custom-call.3 | solution.py:96
  318.3 88.9 %all-reduce.28.cloned.1.call-done = (f32[4,1,128,512]{3,2,0,1:T(8,128)}, f32[4,1,128,512]{3,2,0,1:T(8,128)}) async-done(((f32[4,1,128,512]{3,2,0,1:T(8,128)}, f32[4,1,128,512]{3,2,0,1:T(8,128)}), (f32[4,1,128,512]{3,2,0,1:T(8,128)}, f32[4,1,128,512]{3,2,0,1:T(8,128)})) %all-reduce.28.cloned.1.call-update) | async-done | bytes 2097168 | tf_op jit(solution)/shard_map/psum | solution.py:19
  418.5 44.2 %collective-permute-done = f32[4,128,8,128]{3,1,2,0:T(8,128)} collective-permute-done((f32[4,128,8,128]{3,1,2,0:T(8,128)}, f32[4,128,8,128]{3,1,2,0:T(8,128)}, u32[]{:S(2)}, u32[]{:S(2)}) %collective-permute-start) | collective-permute-done | bytes 2097184 | tf_op jit(solution)/shard_map/ppermute | solution.py:14
  471.6 42.9 %collective-permute-done.1 = f32[4,128,8,128]{3,1,2,0:T(8,128)S(1)} collective-permute-done((f32[4,128,8,128]{3,1,2,0:T(8,128)}, f32[4,128,8,128]{3,1,2,0:T(8,128)S(1)}, u32[]{:S(2)}, u32[]{:S(2)}) %collective-permute-start.1) | collective-permute-done | bytes 2097184 | tf_op jit(solution)/shard_map/ppermute | solution.py:14
  526.1 41.8 %collective-permute-done.2 = f32[4,128,8,128]{3,1,2,0:T(8,128)} collective-permute-done((f32[4,128,8,128]{3,1,2,0:T(8,128)}, f32[4,128,8,128]{3,1,2,0:T(8,128)}, u32[]{:S(2)}, u32[]{:S(2)}) %collective-permute-start.2) | collective-permute-done | bytes 2097184 | tf_op jit(solution)/shard_map/ppermute | solution.py:14
  575.6 41.9 %collective-permute-done.3 = f32[4,128,8,128]{3,1,2,0:T(8,128)S(1)} collective-permute-done((f32[4,128,8,128]{3,1,2,0:T(8,128)}, f32[4,128,8,128]{3,1,2,0:T(8,128)S(1)}, u32[]{:S(2)}, u32[]{:S(2)}) %collective-permute-start.3) | collective-permute-done | bytes 2097184 | tf_op jit(solution)/shard_map/ppermute | solution.py:14
  626.3 40.2 %collective-permute-done.4 = f32[4,128,8,128]{3,1,2,0:T(8,128)} collective-permute-done((f32[4,128,8,128]{3,1,2,0:T(8,128)}, f32[4,128,8,128]{3,1,2,0:T(8,128)}, u32[]{:S(2)}, u32[]{:S(2)}) %collective-permute-start.4) | collective-permute-done | bytes 2097184 | tf_op jit(solution)/shard_map/ppermute | solution.py:14
  671.0 23.9 %collective-permute-done.5 = f32[4,128,8,128]{3,1,2,0:T(8,128)S(1)} collective-permute-done((f32[4,128,8,128]{3,1,2,0:T(8,128)}, f32[4,128,8,128]{3,1,2,0:T(8,128)S(1)}, u32[]{:S(2)}, u32[]{:S(2)}) %collective-permute-start.5) | collective-permute-done | bytes 2097184 | tf_op jit(solution)/shard_map/ppermute | solution.py:14
  701.3 66.3 %all-reduce.34.cloned.1.call-done = (f32[4,128,1,128]{3,1,2,0:T(8,128)}, f32[4,128,1,128]{3,1,2,0:T(8,128)}, f32[4,128,1,128]{3,1,2,0:T(8,128)}, f32[4,128,1,128]{3,1,2,0:T(8,128)}) async-done(((f32[4,128,1,128]{3,1,2,0:T(8,128)}, f32[4,128,1,128]{3,1,2,0:T(8,128)}, f32[4,128,1,128]{3,1,2,0:T(8,128)}, f32[4,128,1,128]{3,1,2,0:T(8,128)}), (f32[4,128,1,128]{3,1,2,0:T(8,128)}, f32[4,128,1,128]{3,1,2,0:T(8,128)}, ...) | async-done | bytes 1048592 | tf_op jit(solution)/shard_map/psum | solution.py:19
  782.7 83.4 %all-reduce.26.cloned.1.call-done = (f32[128,512]{0,1:T(8,128)}, f32[128,512]{0,1:T(8,128)}, f32[128,512]{0,1:T(8,128)}, f32[128,512]{0,1:T(8,128)}) async-done(((f32[128,512]{0,1:T(8,128)}, f32[128,512]{0,1:T(8,128)}, f32[128,512]{0,1:T(8,128)}, f32[128,512]{0,1:T(8,128)}), (f32[128,512]{0,1:T(8,128)}, f32[128,512]{0,1:T(8,128)}, f32[128,512]{0,1:T(8,128)}, ...) | async-done | bytes 1048592 | tf_op jit(solution)/shard_map/psum | solution.py:19
  903.9 11.7 cholesky.465
  953.0 12.1 cholesky.503
  973.3 12.0 while.7
  986.0 40.1 %custom-call.38 = f32[4,128,128]{1,2,0:T(8,128)S(1)} custom-call(f32[4,128,128]{2,1,0:T(8,128)} %copy-done.17), custom_call_target="InvertDiagBlocksLowerTriangular" | custom-call | tf_op jit(solution)/shard_map/triangular_solve/custom-call.3 | solution.py:96
  1035.8 89.6 %all-reduce.24.cloned.1.call-done = (f32[4,1,128,512]{3,2,0,1:T(8,128)}, f32[4,1,128,512]{3,2,0,1:T(8,128)}) async-done(((f32[4,1,128,512]{3,2,0,1:T(8,128)}, f32[4,1,128,512]{3,2,0,1:T(8,128)}), (f32[4,1,128,512]{3,2,0,1:T(8,128)}, f32[4,1,128,512]{3,2,0,1:T(8,128)})) %all-reduce.24.cloned.1.call-update) | async-done | bytes 2097168 | tf_op jit(solution)/shard_map/psum | solution.py:19
  1134.6 43.9 %collective-permute-done.6 = f32[4,128,8,128]{3,1,2,0:T(8,128)S(1)} collective-permute-done((f32[4,128,8,128]{3,1,2,0:T(8,128)S(1)}, f32[4,128,8,128]{3,1,2,0:T(8,128)S(1)}, u32[]{:S(2)}, u32[]{:S(2)}) %collective-permute-start.6) | collective-permute-done | bytes 2097184 | tf_op jit(solution)/shard_map/ppermute | solution.py:14
  1183.9 42.6 %collective-permute-done.7 = f32[4,128,8,128]{3,1,2,0:T(8,128)S(1)} collective-permute-done((f32[4,128,8,128]{3,1,2,0:T(8,128)S(1)}, f32[4,128,8,128]{3,1,2,0:T(8,128)S(1)}, u32[]{:S(2)}, u32[]{:S(2)}) %collective-permute-start.7) | collective-permute-done | bytes 2097184 | tf_op jit(solution)/shard_map/ppermute | solution.py:14
  1233.9 41.2 %collective-permute-done.8 = f32[4,128,8,128]{3,1,2,0:T(8,128)S(1)} collective-permute-done((f32[4,128,8,128]{3,1,2,0:T(8,128)S(1)}, f32[4,128,8,128]{3,1,2,0:T(8,128)S(1)}, u32[]{:S(2)}, u32[]{:S(2)}) %collective-permute-start.8) | collective-permute-done | bytes 2097184 | tf_op jit(solution)/shard_map/ppermute | solution.py:14
  1279.2 41.1 %collective-permute-done.9 = f32[4,128,8,128]{3,1,2,0:T(8,128)S(1)} collective-permute-done((f32[4,128,8,128]{3,1,2,0:T(8,128)S(1)}, f32[4,128,8,128]{3,1,2,0:T(8,128)S(1)}, u32[]{:S(2)}, u32[]{:S(2)}) %collective-permute-start.9) | collective-permute-done | bytes 2097184 | tf_op jit(solution)/shard_map/ppermute | solution.py:14
  1326.6 38.9 %collective-permute-done.10 = f32[4,128,8,128]{3,1,2,0:T(8,128)S(1)} collective-permute-done((f32[4,128,8,128]{3,1,2,0:T(8,128)S(1)}, f32[4,128,8,128]{3,1,2,0:T(8,128)S(1)}, u32[]{:S(2)}, u32[]{:S(2)}) %collective-permute-start.10) | collective-permute-done | bytes 2097184 | tf_op jit(solution)/shard_map/ppermute | solution.py:14
  1366.5 23.5 %collective-permute-done.11 = f32[4,128,8,128]{3,1,2,0:T(8,128)S(1)} collective-permute-done((f32[4,128,8,128]{3,1,2,0:T(8,128)S(1)}, f32[4,128,8,128]{3,1,2,0:T(8,128)S(1)}, u32[]{:S(2)}, u32[]{:S(2)}) %collective-permute-start.11) | collective-permute-done | bytes 2097184 | tf_op jit(solution)/shard_map/ppermute | solution.py:14
  1392.4 66.3 %all-reduce.32.cloned.1.call-done = (f32[4,128,1,128]{3,1,2,0:T(8,128)}, f32[4,128,1,128]{3,1,2,0:T(8,128)}, f32[4,128,1,128]{3,1,2,0:T(8,128)}, f32[4,128,1,128]{3,1,2,0:T(8,128)}) async-done(((f32[4,128,1,128]{3,1,2,0:T(8,128)}, f32[4,128,1,128]{3,1,2,0:T(8,128)}, f32[4,128,1,128]{3,1,2,0:T(8,128)}, f32[4,128,1,128]{3,1,2,0:T(8,128)}), (f32[4,128,1,128]{3,1,2,0:T(8,128)}, f32[4,128,1,128]{3,1,2,0:T(8,128)}, ...) | async-done | bytes 1048592 | tf_op jit(solution)/shard_map/psum | solution.py:19
  1473.8 83.3 %all-reduce.22.cloned.1.call-done = (f32[128,512]{0,1:T(8,128)}, f32[128,512]{0,1:T(8,128)}, f32[128,512]{0,1:T(8,128)}, f32[128,512]{0,1:T(8,128)}) async-done(((f32[128,512]{0,1:T(8,128)}, f32[128,512]{0,1:T(8,128)}, f32[128,512]{0,1:T(8,128)}, f32[128,512]{0,1:T(8,128)}), (f32[128,512]{0,1:T(8,128)}, f32[128,512]{0,1:T(8,128)}, f32[128,512]{0,1:T(8,128)}, ...) | async-done | bytes 1048592 | tf_op jit(solution)/shard_map/psum | solution.py:19
  1594.9 11.7 cholesky.537
  1644.3 11.9 cholesky.575
  1664.3 12.0 while.8
  1677.1 40.1 %custom-call.42 = f32[4,128,128]{1,2,0:T(8,128)S(1)} custom-call(f32[4,128,128]{2,1,0:T(8,128)} %copy-done.16), custom_call_target="InvertDiagBlocksLowerTriangular" | custom-call | tf_op jit(solution)/shard_map/triangular_solve/custom-call.3 | solution.py:96
  1726.4 89.9 %all-reduce.20.cloned.1.call-done = (f32[4,1,128,512]{3,2,0,1:T(8,128)}, f32[4,1,128,512]{3,2,0,1:T(8,128)}) async-done(((f32[4,1,128,512]{3,2,0,1:T(8,128)}, f32[4,1,128,512]{3,2,0,1:T(8,128)}), (f32[4,1,128,512]{3,2,0,1:T(8,128)}, f32[4,1,128,512]{3,2,0,1:T(8,128)})) %all-reduce.20.cloned.1.call-update) | async-done | bytes 2097168 | tf_op jit(solution)/shard_map/psum | solution.py:19
  (290 shorter events, 441.2 us)
Async XLA Ops:
  7.2 69.4 %all-reduce.36.cloned.1.call-start = ((), (), s32[]{:S(2)}) async-start(), calls=%async_computation.8 | async-start | bytes 2097152 | tf_op jit(solution)/shard_map/psum | solution.py:19
  10.2 160.2 %all-reduce.30.cloned.1.call-start = ((), (), s32[]{:S(2)}) async-start(), calls=%async_computation.5 | async-start | bytes 2097152 | tf_op jit(solution)/shard_map/psum | solution.py:19
  84.0 323.2 %all-reduce.28.cloned.1.call-start = ((), (), s32[]{:S(2)}) async-start(), calls=%async_computation.4 | async-start | bytes 4194304 | tf_op jit(solution)/shard_map/psum | solution.py:19
  311.3 2.4 copy-start.4
  317.3 450.3 %all-reduce.34.cloned.1.call-start = ((), (), s32[]{:S(2)}) async-start(), calls=%async_computation.7 | async-start | bytes 2097152 | tf_op jit(solution)/shard_map/psum | solution.py:19
  409.0 1.6 copy-start
  409.0 1.8 copy-start.1
  416.1 46.6 %collective-permute-start = (f32[4,128,8,128]{3,1,2,0:T(8,128)}, f32[4,128,8,128]{3,1,2,0:T(8,128)}, u32[]{:S(2)}, u32[]{:S(2)}) collective-permute-start(f32[4,128,8,128]{3,1,2,0:T(8,128)} %get-tuple-element.212), channel_id=1, source_target_pairs={{0,96},{8,104},{16,112},{24,120},{32,0},{40,8},{48,16},{56,24},{64... | collective-permute-start | bytes 6291464 | tf_op jit(solution)/shard_map/ppermute | solution.py:14
  467.2 47.2 %collective-permute-start.1 = (f32[4,128,8,128]{3,1,2,0:T(8,128)}, f32[4,128,8,128]{3,1,2,0:T(8,128)S(1)}, u32[]{:S(2)}, u32[]{:S(2)}) collective-permute-start(f32[4,128,8,128]{3,1,2,0:T(8,128)} %get-tuple-element.127), channel_id=1, source_target_pairs={{0,112},{8,120},{16,0},{24,8},{32,16},{40,24},{48,32},{56,40},{64,... | collective-permute-start | bytes 6291464 | tf_op jit(solution)/shard_map/ppermute | solution.py:14
  514.4 1.3 copy-start.15
  520.2 47.8 %collective-permute-start.2 = (f32[4,128,8,128]{3,1,2,0:T(8,128)}, f32[4,128,8,128]{3,1,2,0:T(8,128)}, u32[]{:S(2)}, u32[]{:S(2)}) collective-permute-start(f32[4,128,8,128]{3,1,2,0:T(8,128)} %get-tuple-element.125), channel_id=1, source_target_pairs={{0,120},{8,0},{16,8},{24,16},{32,24},{40,32},{48,40},{56,48},{64,5... | collective-permute-start | bytes 6291464 | tf_op jit(solution)/shard_map/ppermute | solution.py:14
  572.4 45.0 %collective-permute-start.3 = (f32[4,128,8,128]{3,1,2,0:T(8,128)}, f32[4,128,8,128]{3,1,2,0:T(8,128)S(1)}, u32[]{:S(2)}, u32[]{:S(2)}) collective-permute-start(f32[4,128,8,128]{3,1,2,0:T(8,128)} %get-tuple-element.123), channel_id=1, source_target_pairs={{0,4},{1,5},{2,6},{3,7},{4,0},{5,1},{6,2},{7,3},{8,12},{9,13},{10,... | collective-permute-start | bytes 6291464 | tf_op jit(solution)/shard_map/ppermute | solution.py:14
  617.5 1.3 copy-start.14
  623.3 43.2 %collective-permute-start.4 = (f32[4,128,8,128]{3,1,2,0:T(8,128)}, f32[4,128,8,128]{3,1,2,0:T(8,128)}, u32[]{:S(2)}, u32[]{:S(2)}) collective-permute-start(f32[4,128,8,128]{3,1,2,0:T(8,128)} %get-tuple-element.121), channel_id=1, source_target_pairs={{0,6},{1,7},{2,0},{3,1},{4,2},{5,3},{6,4},{7,5},{8,14},{9,15},{10,... | collective-permute-start | bytes 6291464 | tf_op jit(solution)/shard_map/ppermute | solution.py:14
  671.0 23.9 %collective-permute-start.5 = (f32[4,128,8,128]{3,1,2,0:T(8,128)}, f32[4,128,8,128]{3,1,2,0:T(8,128)S(1)}, u32[]{:S(2)}, u32[]{:S(2)}) collective-permute-start(f32[4,128,8,128]{3,1,2,0:T(8,128)} %get-tuple-element.119), channel_id=1, source_target_pairs={{0,7},{1,0},{2,1},{3,2},{4,3},{5,4},{6,5},{7,6},{8,15},{9,8},{10,9... | collective-permute-start | bytes 6291464 | tf_op jit(solution)/shard_map/ppermute | solution.py:14
  694.9 1.3 copy-start.13
  701.3 164.8 %all-reduce.26.cloned.1.call-start = ((), (), s32[]{:S(2)}) async-start(), calls=%async_computation.3 | async-start | bytes 2097152 | tf_op jit(solution)/shard_map/psum | solution.py:19
  779.6 345.9 %all-reduce.24.cloned.1.call-start = ((), (), s32[]{:S(2)}) async-start(), calls=%async_computation.2 | async-start | bytes 4194304 | tf_op jit(solution)/shard_map/psum | solution.py:19
  1027.8 4.2 copy-start.5
  1035.6 423.0 %all-reduce.32.cloned.1.call-start = ((), (), s32[]{:S(2)}) async-start(), calls=%async_computation.6 | async-start | bytes 2097152 | tf_op jit(solution)/shard_map/psum | solution.py:19
  1127.2 1.2 copy-start.2
  1132.2 46.3 %collective-permute-start.6 = (f32[4,128,8,128]{3,1,2,0:T(8,128)S(1)}, f32[4,128,8,128]{3,1,2,0:T(8,128)S(1)}, u32[]{:S(2)}, u32[]{:S(2)}) collective-permute-start(f32[4,128,8,128]{3,1,2,0:T(8,128)S(1)} %get-tuple-element.217), channel_id=1, source_target_pairs={{0,96},{8,104},{16,112},{24,120},{32,0},{40,8},{48,16},{56,24},{64... | collective-permute-start | bytes 6291464 | tf_op jit(solution)/shard_map/ppermute | solution.py:14
  1179.4 47.0 %collective-permute-start.7 = (f32[4,128,8,128]{3,1,2,0:T(8,128)S(1)}, f32[4,128,8,128]{3,1,2,0:T(8,128)S(1)}, u32[]{:S(2)}, u32[]{:S(2)}) collective-permute-start(f32[4,128,8,128]{3,1,2,0:T(8,128)S(1)} %get-tuple-element.117), channel_id=1, source_target_pairs={{0,112},{8,120},{16,0},{24,8},{32,16},{40,24},{48,32},{56,40},{64,... | collective-permute-start | bytes 6291464 | tf_op jit(solution)/shard_map/ppermute | solution.py:14
  1227.4 47.6 %collective-permute-start.8 = (f32[4,128,8,128]{3,1,2,0:T(8,128)S(1)}, f32[4,128,8,128]{3,1,2,0:T(8,128)S(1)}, u32[]{:S(2)}, u32[]{:S(2)}) collective-permute-start(f32[4,128,8,128]{3,1,2,0:T(8,128)S(1)} %get-tuple-element.115), channel_id=1, source_target_pairs={{0,120},{8,0},{16,8},{24,16},{32,24},{40,32},{48,40},{56,48},{64,5... | collective-permute-start | bytes 6291464 | tf_op jit(solution)/shard_map/ppermute | solution.py:14
  1276.0 44.3 %collective-permute-start.9 = (f32[4,128,8,128]{3,1,2,0:T(8,128)S(1)}, f32[4,128,8,128]{3,1,2,0:T(8,128)S(1)}, u32[]{:S(2)}, u32[]{:S(2)}) collective-permute-start(f32[4,128,8,128]{3,1,2,0:T(8,128)S(1)} %get-tuple-element.113), channel_id=1, source_target_pairs={{0,4},{1,5},{2,6},{3,7},{4,0},{5,1},{6,2},{7,3},{8,12},{9,13},{10,... | collective-permute-start | bytes 6291464 | tf_op jit(solution)/shard_map/ppermute | solution.py:14
  1321.3 44.3 %collective-permute-start.10 = (f32[4,128,8,128]{3,1,2,0:T(8,128)S(1)}, f32[4,128,8,128]{3,1,2,0:T(8,128)S(1)}, u32[]{:S(2)}, u32[]{:S(2)}) collective-permute-start(f32[4,128,8,128]{3,1,2,0:T(8,128)S(1)} %get-tuple-element.111), channel_id=1, source_target_pairs={{0,6},{1,7},{2,0},{3,1},{4,2},{5,3},{6,4},{7,5},{8,14},{9,15},{10,... | collective-permute-start | bytes 6291464 | tf_op jit(solution)/shard_map/ppermute | solution.py:14
  1365.5 24.5 %copy-start.12 = (f32[1,4,128,1,8,128]{5,4,3,2,1,0:T(8,128)S(1)}, f32[1,4,128,1,8,128]{5,4,3,2,1,0:T(8,128)}, u32[]{:S(2)}) copy-start(f32[1,4,128,1,8,128]{5,4,3,2,1,0:T(8,128)} %param.14) | copy-start | bytes 6291460
  1366.5 23.6 %collective-permute-start.11 = (f32[4,128,8,128]{3,1,2,0:T(8,128)S(1)}, f32[4,128,8,128]{3,1,2,0:T(8,128)S(1)}, u32[]{:S(2)}, u32[]{:S(2)}) collective-permute-start(f32[4,128,8,128]{3,1,2,0:T(8,128)S(1)} %get-tuple-element.109), channel_id=1, source_target_pairs={{0,7},{1,0},{2,1},{3,2},{4,3},{5,4},{6,5},{7,6},{8,15},{9,8},{10,9... | collective-permute-start | bytes 6291464 | tf_op jit(solution)/shard_map/ppermute | solution.py:14
  1392.3 164.8 %all-reduce.22.cloned.1.call-start = ((), (), s32[]{:S(2)}) async-start(), calls=%async_computation.1 | async-start | bytes 2097152 | tf_op jit(solution)/shard_map/psum | solution.py:19
  1470.7 345.6 %all-reduce.20.cloned.1.call-start = ((), (), s32[]{:S(2)}) async-start(), calls=%async_computation | async-start | bytes 4194304 | tf_op jit(solution)/shard_map/psum | solution.py:19
  1718.9 4.2 copy-start.3
  1726.3 91.8 %copy-start.6 = (f32[512,512]{1,0:T(8,128)}, f32[512,512]{1,0:T(8,128)S(1)}, u32[]{:S(2)}) copy-start(f32[512,512]{1,0:T(8,128)S(1)} %get-tuple-element.221) | copy-start | bytes 3145732
  (9 other events, 7.6 us)
Sparse Core Ops, SparseCore 0:
  11.2 65.3 all-reduce.35
  84.1 86.3 all-reduce.29
  317.4 89.6 all-reduce.27
  701.4 66.1 all-reduce.33
  779.7 86.3 all-reduce.25
  1035.7 89.6 all-reduce.23
  1392.4 66.1 all-reduce.31
  1470.8 86.3 all-reduce.21
  1726.5 89.7 all-reduce.19
where the time goes:
time: 1840 us; the launch traced here: 1830 us
  waiting for transfers between devices  1180 us (64%)
  other arithmetic  413 us (22%)
  local copies, waits for them, and re-layouts  110 us (6%)
  matrix products  58.9 us (3%)
  starting transfers between devices  41.9 us (2%)
  between operations  22.7 us (1%)
    psum x9, waiting for transfers between devices, spread(): return lax.psum(block, axis)  718 us
    ppermute x12, waiting for transfers between devices, shifted(): return lax.ppermute(value, axis, pairs)  466 us
    another operation x44, other arithmetic, factor_local(): factor_block = jnp.linalg.cholesky(diagonal)  242 us
    another operation x7, other arithmetic, factor_local(): lax.linalg.triangular_solve(factor_block, jnp.eye(PANEL, dtype=jnp.float3...  124 us
    ppermute x12, starting transfers between devices, shifted(): return lax.ppermute(value, axis, pairs)  40.5 us
    unnamed x60, local copies, waits for them, and re-layouts  39.2 us
  transfers between devices with their start and end apart: 21, of which 21 were waited for; matrix products, arithmetic and copies ran while one was open for 0% of the time, Pallas kernels for 0%

commit v1 on v0

--- a/solution.py
+++ b/solution.py
@@ -16,7 +16,7 @@
 
 def spread(block, axis, source):
     block = jnp.where(lax.axis_index(axis) == source, block, jnp.zeros_like(block))
-    return lax.psum(block, axis)
+    return jnp.sum(jax.lax.all_gather(block, axis_name=axis), axis=0)
 
 
 def shift_rows(block_data, amount):

time: 1840 us -> 2780 us (1.51)
  waiting for transfers between devices: 1180 us -> 2010 us
  other arithmetic: 413 us -> 531 us
    all_gather x0 -> x30, waiting for transfers between devices: none -> 1530 us  [spread(): return jnp.sum(jax.lax.all_gather(block, axis_name=axis), axis=0)]
    psum x9 -> x0, waiting for transfers between devices: 718 us -> none  [spread(): return lax.psum(block, axis)]
    reduce_sum x0 -> x30, other arithmetic: none -> 112 us  [spread(): return jnp.sum(jax.lax.all_gather(block, axis_name=axis), axis=0)]
  transfers between devices with their start and end apart: 21 -> 42, of which waited for: 21 -> 42; matrix products, arithmetic and copies ran while one was open for 0% -> 4% of each run, Pallas kernels for 0% -> 0%
where the time goes in v1:
time: 2780 us; the launch traced here: 2770 us
  waiting for transfers between devices  2010 us (72%)
  other arithmetic  531 us (19%)
  local copies, waits for them, and re-layouts  106 us (4%)
  matrix products  55.6 us (2%)
  starting transfers between devices  41.4 us (1%)
    all_gather x30, waiting for transfers between devices, spread(): return jnp.sum(jax.lax.all_gather(block, axis_name=axis), axis=0)  1530 us
    ppermute x12, waiting for transfers between devices, shifted(): return lax.ppermute(value, axis, pairs)  481 us
    another operation x44, other arithmetic, factor_local(): factor_block = jnp.linalg.cholesky(diagonal)  242 us
    another operation x7, other arithmetic, factor_local(): lax.linalg.triangular_solve(factor_block, jnp.eye(PANEL, dtype=jnp.float3...  124 us
    reduce_sum x30, other arithmetic, spread(): return jnp.sum(jax.lax.all_gather(block, axis_name=axis), axis=0)  112 us
  transfers between devices with their start and end apart: 42, of which 42 were waited for; matrix products, arithmetic and copies ran while one was open for 4% of the time, Pallas kernels for 0%

profile of v1, /device:TPU:0, one launch (start us, length us, event | category | flops | bytes accessed | tf_op | source)
XLA Modules:
  0.0 2772.4 jit_solution(99220049436442272)
XLA Ops:
  130.8 46.3 %all-gather.55.cloned.1.call-done = f32[16,128,512]{2,1,0:T(8,128)} async-done(((f32[1,128,512]{2,1,0:T(8,128)}), f32[16,128,512]{2,1,0:T(8,128)}) %all-gather.55.cloned.1.call-update) | async-done | bytes 4194320 | tf_op jit(solution)/shard_map/all_gather | solution.py:19
  179.9 50.9 %all-gather.53.cloned.1.call-done = f32[16,128,512]{2,1,0:T(8,128)} async-done(((f32[1,128,512]{2,1,0:T(8,128)}), f32[16,128,512]{2,1,0:T(8,128)}) %all-gather.53.cloned.1.call-update) | async-done | bytes 4194320 | tf_op jit(solution)/shard_map/all_gather | solution.py:19
  233.6 51.1 %all-gather.51.cloned.1.call-done = f32[16,128,512]{2,1,0:T(8,128)} async-done(((f32[1,128,512]{2,1,0:T(8,128)}), f32[16,128,512]{2,1,0:T(8,128)}) %all-gather.51.cloned.1.call-update) | async-done | bytes 4194320 | tf_op jit(solution)/shard_map/all_gather | solution.py:19
  287.5 50.5 %all-gather.49.cloned.1.call-done = f32[16,128,512]{2,1,0:T(8,128)} async-done(((f32[1,128,512]{2,1,0:T(8,128)}), f32[16,128,512]{2,1,0:T(8,128)}) %all-gather.49.cloned.1.call-update) | async-done | bytes 4194320 | tf_op jit(solution)/shard_map/all_gather | solution.py:19
  434.8 39.3 %custom-call.34 = f32[4,128,128]{1,2,0:T(8,128)S(1)} custom-call(f32[4,128,128]{2,1,0:T(8,128)S(1)} %get-tuple-element.28), custom_call_target="InvertDiagBlocksLowerTriangular" | custom-call | tf_op jit(solution)/shard_map/triangular_solve/custom-call.3 | solution.py:96
  482.4 109.6 %all-gather.83.cloned.1.call-done = f32[8192,512]{1,0:T(8,128)} async-done(((f32[512,512]{1,0:T(8,128)}), f32[8192,512]{1,0:T(8,128)}) %all-gather.83.cloned.1.call-update) | async-done | bytes 16777232 | tf_op jit(solution)/shard_map/all_gather | solution.py:19
  599.9 105.6 %all-gather.81.cloned.1.call-done = f32[8192,512]{1,0:T(8,128)} async-done(((f32[512,512]{1,0:T(8,128)}), f32[8192,512]{1,0:T(8,128)}) %all-gather.81.cloned.1.call-update) | async-done | bytes 16777232 | tf_op jit(solution)/shard_map/all_gather | solution.py:19
  723.3 45.2 %collective-permute-done = f32[4,128,8,128]{3,1,2,0:T(8,128)} collective-permute-done((f32[4,128,8,128]{3,1,2,0:T(8,128)}, f32[4,128,8,128]{3,1,2,0:T(8,128)}, u32[]{:S(2)}, u32[]{:S(2)}) %collective-permute-start) | collective-permute-done | bytes 2097184 | tf_op jit(solution)/shard_map/ppermute | solution.py:14
  777.5 44.3 %collective-permute-done.1 = f32[4,128,8,128]{3,1,2,0:T(8,128)S(1)} collective-permute-done((f32[4,128,8,128]{3,1,2,0:T(8,128)}, f32[4,128,8,128]{3,1,2,0:T(8,128)S(1)}, u32[]{:S(2)}, u32[]{:S(2)}) %collective-permute-start.1) | collective-permute-done | bytes 2097184 | tf_op jit(solution)/shard_map/ppermute | solution.py:14
  833.4 43.2 %collective-permute-done.2 = f32[4,128,8,128]{3,1,2,0:T(8,128)} collective-permute-done((f32[4,128,8,128]{3,1,2,0:T(8,128)}, f32[4,128,8,128]{3,1,2,0:T(8,128)}, u32[]{:S(2)}, u32[]{:S(2)}) %collective-permute-start.2) | collective-permute-done | bytes 2097184 | tf_op jit(solution)/shard_map/ppermute | solution.py:14
  884.2 43.2 %collective-permute-done.3 = f32[4,128,8,128]{3,1,2,0:T(8,128)S(1)} collective-permute-done((f32[4,128,8,128]{3,1,2,0:T(8,128)}, f32[4,128,8,128]{3,1,2,0:T(8,128)S(1)}, u32[]{:S(2)}, u32[]{:S(2)}) %collective-permute-start.3) | collective-permute-done | bytes 2097184 | tf_op jit(solution)/shard_map/ppermute | solution.py:14
  936.2 41.6 %collective-permute-done.4 = f32[4,128,8,128]{3,1,2,0:T(8,128)} collective-permute-done((f32[4,128,8,128]{3,1,2,0:T(8,128)}, f32[4,128,8,128]{3,1,2,0:T(8,128)}, u32[]{:S(2)}, u32[]{:S(2)}) %collective-permute-start.4) | collective-permute-done | bytes 2097184 | tf_op jit(solution)/shard_map/ppermute | solution.py:14
  1147.3 39.0 %all-gather.63.cloned.1.call-done = f32[16,128,512]{2,1,0:T(8,128)} async-done(((f32[1,128,512]{2,1,0:T(8,128)}), f32[16,128,512]{2,1,0:T(8,128)}) %all-gather.63.cloned.1.call-update) | async-done | bytes 4194320 | tf_op jit(solution)/shard_map/all_gather | solution.py:19
  1190.7 48.7 %all-gather.61.cloned.1.call-done = f32[16,128,512]{2,1,0:T(8,128)} async-done(((f32[1,128,512]{2,1,0:T(8,128)}), f32[16,128,512]{2,1,0:T(8,128)}) %all-gather.61.cloned.1.call-update) | async-done | bytes 4194320 | tf_op jit(solution)/shard_map/all_gather | solution.py:19
  1244.5 48.6 %all-gather.59.cloned.1.call-done = f32[16,128,512]{2,1,0:T(8,128)} async-done(((f32[1,128,512]{2,1,0:T(8,128)}), f32[16,128,512]{2,1,0:T(8,128)}) %all-gather.59.cloned.1.call-update) | async-done | bytes 4194320 | tf_op jit(solution)/shard_map/all_gather | solution.py:19
  1298.3 48.0 %all-gather.57.cloned.1.call-done = f32[16,128,512]{2,1,0:T(8,128)} async-done(((f32[1,128,512]{2,1,0:T(8,128)}), f32[16,128,512]{2,1,0:T(8,128)}) %all-gather.57.cloned.1.call-update) | async-done | bytes 4194320 | tf_op jit(solution)/shard_map/all_gather | solution.py:19
  1466.4 40.1 %custom-call.38 = f32[4,128,128]{1,2,0:T(8,128)S(1)} custom-call(f32[4,128,128]{2,1,0:T(8,128)} %copy-done.18), custom_call_target="InvertDiagBlocksLowerTriangular" | custom-call | tf_op jit(solution)/shard_map/triangular_solve/custom-call.3 | solution.py:96
  1517.0 110.0 %all-gather.95.cloned.1.call-done = f32[8192,512]{1,0:T(8,128)} async-done(((f32[512,512]{1,0:T(8,128)}), f32[8192,512]{1,0:T(8,128)}) %all-gather.95.cloned.1.call-update) | async-done | bytes 16777232 | tf_op jit(solution)/shard_map/all_gather | solution.py:19
  1635.9 104.6 %all-gather.93.cloned.1.call-done = f32[8192,512]{1,0:T(8,128)} async-done(((f32[512,512]{1,0:T(8,128)}), f32[8192,512]{1,0:T(8,128)}) %all-gather.93.cloned.1.call-update) | async-done | bytes 16777232 | tf_op jit(solution)/shard_map/all_gather | solution.py:19
  1757.8 44.9 %collective-permute-done.6 = f32[4,128,8,128]{3,1,2,0:T(8,128)S(1)} collective-permute-done((f32[4,128,8,128]{3,1,2,0:T(8,128)S(1)}, f32[4,128,8,128]{3,1,2,0:T(8,128)S(1)}, u32[]{:S(2)}, u32[]{:S(2)}) %collective-permute-start.6) | collective-permute-done | bytes 2097184 | tf_op jit(solution)/shard_map/ppermute | solution.py:14
  1808.3 44.0 %collective-permute-done.7 = f32[4,128,8,128]{3,1,2,0:T(8,128)S(1)} collective-permute-done((f32[4,128,8,128]{3,1,2,0:T(8,128)S(1)}, f32[4,128,8,128]{3,1,2,0:T(8,128)S(1)}, u32[]{:S(2)}, u32[]{:S(2)}) %collective-permute-start.7) | collective-permute-done | bytes 2097184 | tf_op jit(solution)/shard_map/ppermute | solution.py:14
  1858.9 43.1 %collective-permute-done.8 = f32[4,128,8,128]{3,1,2,0:T(8,128)S(1)} collective-permute-done((f32[4,128,8,128]{3,1,2,0:T(8,128)S(1)}, f32[4,128,8,128]{3,1,2,0:T(8,128)S(1)}, u32[]{:S(2)}, u32[]{:S(2)}) %collective-permute-start.8) | collective-permute-done | bytes 2097184 | tf_op jit(solution)/shard_map/ppermute | solution.py:14
  1906.2 43.0 %collective-permute-done.9 = f32[4,128,8,128]{3,1,2,0:T(8,128)S(1)} collective-permute-done((f32[4,128,8,128]{3,1,2,0:T(8,128)S(1)}, f32[4,128,8,128]{3,1,2,0:T(8,128)S(1)}, u32[]{:S(2)}, u32[]{:S(2)}) %collective-permute-start.9) | collective-permute-done | bytes 2097184 | tf_op jit(solution)/shard_map/ppermute | solution.py:14
  1953.6 40.9 %collective-permute-done.10 = f32[4,128,8,128]{3,1,2,0:T(8,128)S(1)} collective-permute-done((f32[4,128,8,128]{3,1,2,0:T(8,128)S(1)}, f32[4,128,8,128]{3,1,2,0:T(8,128)S(1)}, u32[]{:S(2)}, u32[]{:S(2)}) %collective-permute-start.10) | collective-permute-done | bytes 2097184 | tf_op jit(solution)/shard_map/ppermute | solution.py:14
  2023.3 27.0 all-gather.103.cloned.1.call-done
  2155.9 38.9 %all-gather.71.cloned.1.call-done = f32[16,128,512]{2,1,0:T(8,128)} async-done(((f32[1,128,512]{2,1,0:T(8,128)}), f32[16,128,512]{2,1,0:T(8,128)}) %all-gather.71.cloned.1.call-update) | async-done | bytes 4194320 | tf_op jit(solution)/shard_map/all_gather | solution.py:19
  2199.3 48.7 %all-gather.69.cloned.1.call-done = f32[16,128,512]{2,1,0:T(8,128)} async-done(((f32[1,128,512]{2,1,0:T(8,128)}), f32[16,128,512]{2,1,0:T(8,128)}) %all-gather.69.cloned.1.call-update) | async-done | bytes 4194320 | tf_op jit(solution)/shard_map/all_gather | solution.py:19
  2253.1 48.6 %all-gather.67.cloned.1.call-done = f32[16,128,512]{2,1,0:T(8,128)} async-done(((f32[1,128,512]{2,1,0:T(8,128)}), f32[16,128,512]{2,1,0:T(8,128)}) %all-gather.67.cloned.1.call-update) | async-done | bytes 4194320 | tf_op jit(solution)/shard_map/all_gather | solution.py:19
  2306.8 48.1 %all-gather.65.cloned.1.call-done = f32[16,128,512]{2,1,0:T(8,128)} async-done(((f32[1,128,512]{2,1,0:T(8,128)}), f32[16,128,512]{2,1,0:T(8,128)}) %all-gather.65.cloned.1.call-update) | async-done | bytes 4194320 | tf_op jit(solution)/shard_map/all_gather | solution.py:19
  2474.5 40.1 %custom-call.42 = f32[4,128,128]{1,2,0:T(8,128)S(1)} custom-call(f32[4,128,128]{2,1,0:T(8,128)} %copy-done.19), custom_call_target="InvertDiagBlocksLowerTriangular" | custom-call | tf_op jit(solution)/shard_map/triangular_solve/custom-call.3 | solution.py:96
  2524.7 110.5 %all-gather.107.cloned.1.call-done = f32[8192,512]{1,0:T(8,128)} async-done(((f32[512,512]{1,0:T(8,128)}), f32[8192,512]{1,0:T(8,128)}) %all-gather.107.cloned.1.call-update) | async-done | bytes 16777232 | tf_op jit(solution)/shard_map/all_gather | solution.py:19
  2643.1 105.6 %all-gather.105.cloned.1.call-done = f32[8192,512]{1,0:T(8,128)} async-done(((f32[512,512]{1,0:T(8,128)}), f32[8192,512]{1,0:T(8,128)}) %all-gather.105.cloned.1.call-update) | async-done | bytes 16777232 | tf_op jit(solution)/shard_map/all_gather | solution.py:19
  (390 shorter events, 986.5 us)
Async XLA Ops:
  10.2 56.1 %all-gather.77.cloned.1.call-start = ((), (), s32[]{:S(2)}) async-start(), calls=%async_computation.14 | async-start | bytes 2359296 | tf_op jit(solution)/shard_map/all_gather | solution.py:19
  11.0 83.4 %all-gather.75.cloned.1.call-start = ((), (), s32[]{:S(2)}) async-start(), calls=%async_computation.13 | async-start | bytes 2359296 | tf_op jit(solution)/shard_map/all_gather | solution.py:19
  11.7 110.6 %all-gather.73.cloned.1.call-start = ((), (), s32[]{:S(2)}) async-start(), calls=%async_computation.12 | async-start | bytes 2359296 | tf_op jit(solution)/shard_map/all_gather | solution.py:19
  12.3 164.9 %all-gather.55.cloned.1.call-start = ((), (), s32[]{:S(2)}) async-start(), calls=%async_computation.3 | async-start | bytes 4456448 | tf_op jit(solution)/shard_map/all_gather | solution.py:19
  125.2 105.6 %all-gather.53.cloned.1.call-start = ((), (), s32[]{:S(2)}) async-start(), calls=%async_computation.2 | async-start | bytes 4456448 | tf_op jit(solution)/shard_map/all_gather | solution.py:19
  126.3 158.5 %all-gather.51.cloned.1.call-start = ((), (), s32[]{:S(2)}) async-start(), calls=%async_computation.1 | async-start | bytes 4456448 | tf_op jit(solution)/shard_map/all_gather | solution.py:19
  127.3 210.7 %all-gather.49.cloned.1.call-start = ((), (), s32[]{:S(2)}) async-start(), calls=%async_computation | async-start | bytes 4456448 | tf_op jit(solution)/shard_map/all_gather | solution.py:19
  128.4 463.6 %all-gather.83.cloned.1.call-start = ((), (), s32[]{:S(2)}) async-start(), calls=%async_computation.17 | async-start | bytes 17825792 | tf_op jit(solution)/shard_map/all_gather | solution.py:19
  480.9 224.6 %all-gather.81.cloned.1.call-start = ((), (), s32[]{:S(2)}) async-start(), calls=%async_computation.16 | async-start | bytes 17825792 | tf_op jit(solution)/shard_map/all_gather | solution.py:19
  481.5 559.8 %all-gather.91.cloned.1.call-start = ((), (), s32[]{:S(2)}) async-start(), calls=%async_computation.21 | async-start | bytes 2359296 | tf_op jit(solution)/shard_map/all_gather | solution.py:19
  773.0 48.8 %collective-permute-start.1 = (f32[4,128,8,128]{3,1,2,0:T(8,128)}, f32[4,128,8,128]{3,1,2,0:T(8,128)S(1)}, u32[]{:S(2)}, u32[]{:S(2)}) collective-permute-start(f32[4,128,8,128]{3,1,2,0:T(8,128)} %get-tuple-element.105), channel_id=1, source_target_pairs={{0,112},{8,120},{16,0},{24,8},{32,16},{40,24},{48,32},{56,40},{64,... | collective-permute-start | bytes 6291464 | tf_op jit(solution)/shard_map/ppermute | solution.py:14
  827.6 49.0 %collective-permute-start.2 = (f32[4,128,8,128]{3,1,2,0:T(8,128)}, f32[4,128,8,128]{3,1,2,0:T(8,128)}, u32[]{:S(2)}, u32[]{:S(2)}) collective-permute-start(f32[4,128,8,128]{3,1,2,0:T(8,128)} %get-tuple-element.103), channel_id=1, source_target_pairs={{0,120},{8,0},{16,8},{24,16},{32,24},{40,32},{48,40},{56,48},{64,5... | collective-permute-start | bytes 6291464 | tf_op jit(solution)/shard_map/ppermute | solution.py:14
  1012.5 56.8 %all-gather.89.cloned.1.call-start = ((), (), s32[]{:S(2)}) async-start(), calls=%async_computation.20 | async-start | bytes 2359296 | tf_op jit(solution)/shard_map/all_gather | solution.py:19
  1013.1 84.3 %all-gather.87.cloned.1.call-start = ((), (), s32[]{:S(2)}) async-start(), calls=%async_computation.19 | async-start | bytes 2359296 | tf_op jit(solution)/shard_map/all_gather | solution.py:19
  1013.9 111.4 %all-gather.85.cloned.1.call-start = ((), (), s32[]{:S(2)}) async-start(), calls=%async_computation.18 | async-start | bytes 2359296 | tf_op jit(solution)/shard_map/all_gather | solution.py:19
  1014.4 171.9 %all-gather.63.cloned.1.call-start = ((), (), s32[]{:S(2)}) async-start(), calls=%async_computation.7 | async-start | bytes 4456448 | tf_op jit(solution)/shard_map/all_gather | solution.py:19
  1134.4 105.1 %all-gather.61.cloned.1.call-start = ((), (), s32[]{:S(2)}) async-start(), calls=%async_computation.6 | async-start | bytes 4456448 | tf_op jit(solution)/shard_map/all_gather | solution.py:19
  1138.0 155.1 %all-gather.59.cloned.1.call-start = ((), (), s32[]{:S(2)}) async-start(), calls=%async_computation.5 | async-start | bytes 4456448 | tf_op jit(solution)/shard_map/all_gather | solution.py:19
  1141.7 204.6 %all-gather.57.cloned.1.call-start = ((), (), s32[]{:S(2)}) async-start(), calls=%async_computation.4 | async-start | bytes 4456448 | tf_op jit(solution)/shard_map/all_gather | solution.py:19
  1144.3 482.7 %all-gather.95.cloned.1.call-start = ((), (), s32[]{:S(2)}) async-start(), calls=%async_computation.23 | async-start | bytes 17825792 | tf_op jit(solution)/shard_map/all_gather | solution.py:19
  1516.0 224.6 %all-gather.93.cloned.1.call-start = ((), (), s32[]{:S(2)}) async-start(), calls=%async_computation.22 | async-start | bytes 17825792 | tf_op jit(solution)/shard_map/all_gather | solution.py:19
  1516.6 533.7 %all-gather.103.cloned.1.call-start = ((), (), s32[]{:S(2)}) async-start(), calls=%async_computation.27 | async-start | bytes 2359296 | tf_op jit(solution)/shard_map/all_gather | solution.py:19
  1853.2 48.8 %collective-permute-start.8 = (f32[4,128,8,128]{3,1,2,0:T(8,128)S(1)}, f32[4,128,8,128]{3,1,2,0:T(8,128)S(1)}, u32[]{:S(2)}, u32[]{:S(2)}) collective-permute-start(f32[4,128,8,128]{3,1,2,0:T(8,128)S(1)} %get-tuple-element.93), channel_id=1, source_target_pairs={{0,120},{8,0},{16,8},{24,16},{32,24},{40,32},{48,40},{56,48},{64,5... | collective-permute-start | bytes 6291464 | tf_op jit(solution)/shard_map/ppermute | solution.py:14
  2021.2 56.6 %all-gather.101.cloned.1.call-start = ((), (), s32[]{:S(2)}) async-start(), calls=%async_computation.26 | async-start | bytes 2359296 | tf_op jit(solution)/shard_map/all_gather | solution.py:19
  2022.0 83.9 %all-gather.99.cloned.1.call-start = ((), (), s32[]{:S(2)}) async-start(), calls=%async_computation.25 | async-start | bytes 2359296 | tf_op jit(solution)/shard_map/all_gather | solution.py:19
  2022.7 111.1 %all-gather.97.cloned.1.call-start = ((), (), s32[]{:S(2)}) async-start(), calls=%async_computation.24 | async-start | bytes 2359296 | tf_op jit(solution)/shard_map/all_gather | solution.py:19
  2023.3 171.6 %all-gather.71.cloned.1.call-start = ((), (), s32[]{:S(2)}) async-start(), calls=%async_computation.11 | async-start | bytes 4456448 | tf_op jit(solution)/shard_map/all_gather | solution.py:19
  2142.9 105.1 %all-gather.69.cloned.1.call-start = ((), (), s32[]{:S(2)}) async-start(), calls=%async_computation.10 | async-start | bytes 4456448 | tf_op jit(solution)/shard_map/all_gather | solution.py:19
  2146.6 155.1 %all-gather.67.cloned.1.call-start = ((), (), s32[]{:S(2)}) async-start(), calls=%async_computation.9 | async-start | bytes 4456448 | tf_op jit(solution)/shard_map/all_gather | solution.py:19
  2150.2 204.7 %all-gather.65.cloned.1.call-start = ((), (), s32[]{:S(2)}) async-start(), calls=%async_computation.8 | async-start | bytes 4456448 | tf_op jit(solution)/shard_map/all_gather | solution.py:19
  2152.9 482.3 %all-gather.107.cloned.1.call-start = ((), (), s32[]{:S(2)}) async-start(), calls=%async_computation.29 | async-start | bytes 17825792 | tf_op jit(solution)/shard_map/all_gather | solution.py:19
  2524.2 224.6 %all-gather.105.cloned.1.call-start = ((), (), s32[]{:S(2)}) async-start(), calls=%async_computation.28 | async-start | bytes 17825792 | tf_op jit(solution)/shard_map/all_gather | solution.py:19
  (32 other events, 618.9 us)
Sparse Core Ops, SparseCore 0:
  10.3 27.8 all-gather.78
  40.5 25.7 all-gather.76
  68.6 25.7 all-gather.74
  96.5 25.7 all-gather.72
  125.3 51.7 all-gather.54
  179.7 51.0 all-gather.52
  233.6 51.1 all-gather.50
  286.9 51.1 all-gather.48
  481.0 110.9 all-gather.82
  594.6 110.8 all-gather.80
  1012.6 28.6 all-gather.90
  1043.5 25.7 all-gather.88
  1071.6 25.7 all-gather.86
  1099.5 25.7 all-gather.84
  1134.5 51.7 all-gather.62
  1188.3 51.0 all-gather.60
  1242.0 51.1 all-gather.58
  1295.1 51.0 all-gather.56
  1516.1 110.8 all-gather.94
  1629.6 110.8 all-gather.92
  2021.3 28.9 all-gather.102
  2052.0 25.7 all-gather.100
  2080.1 25.7 all-gather.98
  2108.1 25.7 all-gather.96
  2143.0 51.7 all-gather.70
  2196.8 51.0 all-gather.68
  2250.5 51.1 all-gather.66
  2303.8 51.1 all-gather.64
  2524.3 110.8 all-gather.106
  2637.8 110.8 all-gather.104
